TPU v7x, 128 devices: a whole 4x4x4 slice. The times are simulated.
128 devices in a mesh: vel: 8 (over y, z_lo), space: 16 (over x, z_hi, core).
Axes of the slice: x: 4, y: 4, z: 4 (z_hi: 2, z_lo: 2; z = z_hi * 2 + z_lo), core: 2. Of those that a mesh axis runs over, the one named last changes fastest.
Arguments:
- density: float32 [1024, 64, 8, 128], P('vel', 'space'), may hold values from -6 to 6
- limiter: int32 [64, 8, 128], P('space'), may hold values from 0 to 2
- heading: int32 [1024], P('vel'), may hold values from 0 to 1
- courant: float32 [1024], P('vel'), may hold values from 0.1 to 0.9
- kernel_slices: bfloat16 [16, 1024, 1024], P('space', None, 'vel'), may hold values from -0.046875 to 0.046875
Outputs:
- transported: float32 [1024, 64, 8, 128], P('vel', 'space')
- collision: float32 [1024, 64, 8, 128], P('vel', 'space')
Inputs may be any that keep to these rules, and one draw needn't show every extreme that they name: `limiter`: 0 no slope, 1 minmod slope, 2 central slope.
All inputs are finite; a program needn't handle non-finite values.
Results may differ from a plain program's by a relative error of at most 0.0041.
Values may be sent and summed in bfloat16 or wider, within the bound.
No kernel may reach another device: no remote copies, remote signals or barrier semaphores. Data moves between devices by JAX's collectives and lax.ppermute only.
A program may use at most 128 MiB of HBM per device.

v0:
```python
import jax
import jax.numpy as jnp
from jax import lax
from jax.sharding import PartitionSpec as P

V = 1024
SLICES = 16


def extended(shard, sides, width):
    for axis, dim in sides:
        size, length = (lax.axis_size(axis), shard.shape[dim])
        up = [(i, (i + 1) % size) for i in range(size - 1)]
        down = [(j, i) for i, j in up]
        last = lax.slice_in_dim(shard, length - width, length, axis=dim)
        first = lax.slice_in_dim(shard, 0, width, axis=dim)
        before = lax.ppermute(last, axis, up)
        after = lax.ppermute(first, axis, down)
        shard = jnp.concatenate([before, shard, after], axis=dim)
    return shard


def limited_slopes(left_diff, right_diff, limiter):
    minmod_slope = jnp.where(
        left_diff * right_diff > 0,
        jnp.sign(left_diff) * jnp.minimum(jnp.abs(left_diff), jnp.abs(right_diff)),
        jnp.zeros_like(left_diff),
    )
    central = 0.5 * (left_diff + right_diff)
    codes = limiter[None]
    return jnp.where(
        codes == 1, minmod_slope, jnp.where(codes == 2, central, jnp.zeros_like(central))
    )


def make_fold(source, totals, pieces):
    stride = V // SLICES

    def one_slice(counter, running):
        matrix = lax.dynamic_index_in_dim(pieces, counter, 0, keepdims=False)
        projected = lax.dot_general(
            matrix, source, (((0,), (0,)), ((), ())), preferred_element_type=jnp.float32
        )
        weight = lax.dynamic_index_in_dim(source, counter * stride, 0, keepdims=True).astype(
            jnp.float32
        )
        return running + weight * projected

    return lax.fori_loop(0, pieces.shape[0], one_slice, totals)


def local(density, limiter, heading, courant, kernel_slices):
    padded = extended(density, (("space", 1),), 1)
    left_diff = density - padded[:, :-2]
    right_diff = padded[:, 2:] - density
    slopes = limited_slopes(left_diff, right_diff, limiter)
    upwind = (2 * heading - 1).astype(jnp.float32)[:, None, None, None]
    rebuilt = density + 0.5 * upwind * slopes
    rebuilt_pad = extended(rebuilt, (("space", 1),), 1)
    forward = (heading == 1)[:, None, None, None]
    upstream = jnp.where(forward, rebuilt_pad[:, :-2], rebuilt_pad[:, 2:])
    transported = density - courant[:, None, None, None] * (rebuilt - upstream)
    flattened = transported.astype(jnp.bfloat16).reshape(density.shape[0], -1)
    columns = lax.all_to_all(flattened, "vel", split_axis=1, concat_axis=0, tiled=True)
    full_slices = lax.all_gather(kernel_slices, "vel", axis=2, tiled=True)
    initial = jnp.zeros(columns.shape, jnp.float32)
    summed = make_fold(columns, initial, lax.all_gather(full_slices, "space", axis=0, tiled=True))
    restored = lax.all_to_all(summed, "vel", split_axis=0, concat_axis=1, tiled=True)
    return (transported, restored.reshape(density.shape))


def solution(mesh):
    return jax.shard_map(
        local,
        mesh=mesh,
        in_specs=(
            P("vel", "space", None, None),
            P("space", None, None),
            P("vel"),
            P("vel"),
            P("space", None, "vel"),
        ),
        out_specs=(P("vel", "space", None, None), P("vel", "space", None, None)),
        check_vma=False,
    )
```

profile of v0, /device:TPU:1, one launch (start us, length us, event | category | flops | bytes accessed | tf_op | source)
XLA Modules:
  0.0 379.8 jit_solution(10808552207556664224)
XLA Ops:
  7.9 61.5 %all-gather.3.cloned.1.call-done = bf16[1,1024,1024]{2,1,0:T(8,128)(2,1)} async-done(((bf16[1,1024,128]{2,1,0:T(8,128)(2,1)}), bf16[1,1024,1024]{2,1,0:T(8,128)(2,1)}) %all-gather.3.cloned.1.call-update) | async-done | bytes 2097168 | tf_op jit(solution)/shard_map/all_gather | solution.py:65
  69.5 2.0 copy.16
  71.6 6.6 %collective-permute-start = (f32[128,1,8,128]{0,3,2,1:T(8,128)S(1)}, f32[128,1,8,128]{0,3,2,1:T(8,128)S(1)}, u32[]{:S(2)}, u32[]{:S(2)}) collective-permute-start(f32[128,1,8,128]{0,3,2,1:T(8,128)S(1)} %get-tuple-element.111), channel_id=1, source_target_pairs={{0,1},{1,2},{2,3},{3,4},{4,5},{5,6},{6,7},{7,8},{8,9},{9,10},{10,1... | collective-permute-start | bytes 1572872 | tf_op jit(solution)/shard_map/ppermute | solution.py:17
  78.2 1.9 collective-permute-start.1
  80.2 11.6 %collective-permute-done = f32[128,1,8,128]{0,3,2,1:T(8,128)S(1)} collective-permute-done((f32[128,1,8,128]{0,3,2,1:T(8,128)S(1)}, f32[128,1,8,128]{0,3,2,1:T(8,128)S(1)}, u32[]{:S(2)}, u32[]{:S(2)}) %collective-permute-start) | collective-permute-done | bytes 524320 | tf_op jit(solution)/shard_map/ppermute | solution.py:17
  93.8 5.9 %collective-permute-start.2 = (f32[128,1,8,128]{0,3,2,1:T(8,128)S(1)}, f32[128,1,8,128]{0,3,2,1:T(8,128)S(1)}, u32[]{:S(2)}, u32[]{:S(2)}) collective-permute-start(f32[128,1,8,128]{0,3,2,1:T(8,128)S(1)} %get-tuple-element.109), channel_id=1, source_target_pairs={{0,1},{1,2},{2,3},{3,4},{4,5},{5,6},{6,7},{7,8},{8,9},{9,10},{10,1... | collective-permute-start | bytes 1572872 | tf_op jit(solution)/shard_map/ppermute | solution.py:17
  99.7 1.9 collective-permute-start.3
  101.6 26.6 %collective-permute-done.2 = f32[128,1,8,128]{0,3,2,1:T(8,128)S(1)} collective-permute-done((f32[128,1,8,128]{0,3,2,1:T(8,128)S(1)}, f32[128,1,8,128]{0,3,2,1:T(8,128)S(1)}, u32[]{:S(2)}, u32[]{:S(2)}) %collective-permute-start.2) | collective-permute-done | bytes 524320 | tf_op jit(solution)/shard_map/ppermute | solution.py:17
  131.4 3.6 all-to-all-start
  135.0 10.2 %all-to-all-done = bf16[128,8,512]{2,0,1:T(8,128)(2,1)S(1)} async-done(((bf16[128,8,512]{2,0,1:T(8,128)(2,1)}), bf16[128,8,512]{2,0,1:T(8,128)(2,1)S(1)}, u32[]{:S(2)}, u32[]{:S(2)}) %all-to-all-start) | async-done | bytes 1048608 | tf_op jit(solution)/shard_map/all_to_all | solution.py:64
  145.2 135.5 %all-gather.5.cloned.1.call-done = bf16[16,1024,1024]{2,1,0:T(8,128)(2,1)} async-done(((bf16[1,1024,1024]{2,1,0:T(8,128)(2,1)}), bf16[16,1024,1024]{2,1,0:T(8,128)(2,1)}) %all-gather.5.cloned.1.call-update) | async-done | bytes 33554448 | tf_op jit(solution)/shard_map/all_gather | solution.py:67
  280.7 51.4 %while.14 = (s32[]{:T(128)}, f32[1024,512]{1,0:T(8,128)S(1)}, bf16[1024,512]{1,0:T(8,128)(2,1)S(1)}, bf16[16,1024,1024]{2,1,0:T(8,128)(2,1)}, s32[]{:T(128)}, /*index=5*/s32[]{:T(128)}, s32[]{:T(128)}, s32[]{:T(128)}) while((s32[]{:T(128)}, f32[1024,512]{1,0:T(8,128)S(1)}, bf16[1024,512]{1,0:T(8,128)(2,1)S(1)}, ...), condition=%wide.region_1.2_spmd.clone, body=%wide.region_0.1_spmd.clone.sunk | while | flops 1075315200 | bytes 7345809 | solution.py:49
  280.7 3.2 select_add_fusion.2
  283.9 3.2 select_add_fusion.2
  287.1 3.2 select_add_fusion.2
  290.4 3.2 select_add_fusion.2
  293.6 3.2 select_add_fusion.2
  296.8 3.2 select_add_fusion.2
  300.0 3.2 select_add_fusion.2
  303.2 3.2 select_add_fusion.2
  306.4 3.2 select_add_fusion.2
  309.7 3.2 select_add_fusion.2
  312.9 3.2 select_add_fusion.2
  316.1 3.2 select_add_fusion.2
  319.3 3.2 select_add_fusion.2
  322.5 3.2 select_add_fusion.2
  325.7 3.2 select_add_fusion.2
  329.0 3.2 select_add_fusion.2
  333.4 4.5 %all-to-all-start.1 = ((f32[8,128,512]{2,1,0:T(8,128)}), f32[8,128,512]{2,1,0:T(8,128)}, u32[]{:S(2)}, u32[]{:S(2)}) async-start(f32[8,128,512]{2,1,0:T(8,128)} %bitcast.23), calls=%async_computation.1 | async-start | bytes 4194304 | tf_op jit(solution)/shard_map/all_to_all | solution.py:68
  337.9 2.0 copy.19
  339.9 29.2 %all-to-all-done.1 = f32[8,128,512]{2,1,0:T(8,128)} async-done(((f32[8,128,512]{2,1,0:T(8,128)}), f32[8,128,512]{2,1,0:T(8,128)}, u32[]{:S(2)}, u32[]{:S(2)}) %all-to-all-start.1) | async-done | bytes 2097184 | tf_op jit(solution)/shard_map/all_to_all | solution.py:68
  371.0 2.0 copy.20
  (42 shorter events, 9.4 us)
Async XLA Ops:
  7.2 62.3 %all-gather.3.cloned.1.call-start = ((), (), s32[]{:S(2)}) async-start(), calls=%async_computation.2 | async-start | bytes 2359296 | tf_op jit(solution)/shard_map/all_gather | solution.py:65
  7.9 272.8 %all-gather.5.cloned.1.call-start = ((), (), s32[]{:S(2)}) async-start(), calls=%async_computation.3 | async-start | bytes 35651584 | tf_op jit(solution)/shard_map/all_gather | solution.py:67
  71.5 8.6 %copy-start.4 = (s32[128]{0:T(128)S(1)}, s32[128]{0:T(128)}, u32[]{:S(2)}) copy-start(s32[128]{0:T(128)} %param.9) | copy-start | bytes 1540
  71.5 8.7 %copy-start.2 = (s32[4,8,128]{2,1,0:T(8,128)S(1)}, s32[4,8,128]{2,1,0:T(8,128)}, u32[]{:S(2)}) copy-start(s32[4,8,128]{2,1,0:T(8,128)} %param.8) | copy-start | bytes 49156
  71.6 20.2 %collective-permute-start = (f32[128,1,8,128]{0,3,2,1:T(8,128)S(1)}, f32[128,1,8,128]{0,3,2,1:T(8,128)S(1)}, u32[]{:S(2)}, u32[]{:S(2)}) collective-permute-start(f32[128,1,8,128]{0,3,2,1:T(8,128)S(1)} %get-tuple-element.111), channel_id=1, source_target_pairs={{0,1},{1,2},{2,3},{3,4},{4,5},{5,6},{6,7},{7,8},{8,9},{9,10},{10,1... | collective-permute-start | bytes 1572872 | tf_op jit(solution)/shard_map/ppermute | solution.py:17
  78.2 13.6 %collective-permute-start.1 = (f32[128,1,8,128]{0,3,2,1:T(8,128)S(1)}, f32[128,1,8,128]{0,3,2,1:T(8,128)S(1)}, u32[]{:S(2)}, u32[]{:S(2)}) collective-permute-start(f32[128,1,8,128]{0,3,2,1:T(8,128)S(1)} %get-tuple-element.112), channel_id=1, source_target_pairs={{1,0},{2,1},{3,2},{4,3},{5,4},{6,5},{7,6},{8,7},{9,8},{10,9},{11,1... | collective-permute-start | bytes 1572872 | tf_op jit(solution)/shard_map/ppermute | solution.py:18
  93.7 34.5 %copy-start.3 = (f32[128]{0:T(128)S(1)}, f32[128]{0:T(128)}, u32[]{:S(2)}) copy-start(f32[128]{0:T(128)} %param.10) | copy-start | bytes 1540
  93.8 34.4 %collective-permute-start.2 = (f32[128,1,8,128]{0,3,2,1:T(8,128)S(1)}, f32[128,1,8,128]{0,3,2,1:T(8,128)S(1)}, u32[]{:S(2)}, u32[]{:S(2)}) collective-permute-start(f32[128,1,8,128]{0,3,2,1:T(8,128)S(1)} %get-tuple-element.109), channel_id=1, source_target_pairs={{0,1},{1,2},{2,3},{3,4},{4,5},{5,6},{6,7},{7,8},{8,9},{9,10},{10,1... | collective-permute-start | bytes 1572872 | tf_op jit(solution)/shard_map/ppermute | solution.py:17
  99.7 28.5 %collective-permute-start.3 = (f32[128,1,8,128]{0,3,2,1:T(8,128)S(1)}, f32[128,1,8,128]{0,3,2,1:T(8,128)S(1)}, u32[]{:S(2)}, u32[]{:S(2)}) collective-permute-start(f32[128,1,8,128]{0,3,2,1:T(8,128)S(1)} %get-tuple-element.110), channel_id=1, source_target_pairs={{1,0},{2,1},{3,2},{4,3},{5,4},{6,5},{7,6},{8,7},{9,8},{10,9},{11,1... | collective-permute-start | bytes 1572872 | tf_op jit(solution)/shard_map/ppermute | solution.py:18
  131.4 13.8 %all-to-all-start = ((bf16[128,8,512]{2,0,1:T(8,128)(2,1)}), bf16[128,8,512]{2,0,1:T(8,128)(2,1)S(1)}, u32[]{:S(2)}, u32[]{:S(2)}) async-start(bf16[128,8,512]{2,0,1:T(8,128)(2,1)} %copy.17), calls=%async_computation | async-start | bytes 2097152 | tf_op jit(solution)/shard_map/all_to_all | solution.py:64
  332.1 1.3 copy-start.1
  333.4 4.5 %copy-start = (f32[128,4,8,128]{0,3,2,1:T(8,128)S(1)}, f32[128,4,8,128]{0,3,2,1:T(8,128)}, u32[]{:S(2)}) copy-start(f32[128,4,8,128]{0,3,2,1:T(8,128)} %get-tuple-element.108) | copy-start | bytes 6291460
  333.4 35.7 %all-to-all-start.1 = ((f32[8,128,512]{2,1,0:T(8,128)}), f32[8,128,512]{2,1,0:T(8,128)}, u32[]{:S(2)}, u32[]{:S(2)}) async-start(f32[8,128,512]{2,1,0:T(8,128)} %bitcast.23), calls=%async_computation.1 | async-start | bytes 4194304 | tf_op jit(solution)/shard_map/all_to_all | solution.py:68
Sparse Core Ops, SparseCore 0:
  9.6 59.8 all-gather.2
  71.8 208.8 all-gather.4
where the time goes:
time: 381 us; the launch traced here: 380 us
  waiting for transfers between devices  275 us (72%)
  matrix products  50.7 us (13%)
  starting transfers between devices  24.5 us (6%)
  between operations  14.2 us (4%)
  local copies, waits for them, and re-layouts  10.6 us (3%)
  other arithmetic  3.97 us (1%)
    all_gather x1, waiting for transfers between devices, local(): lax.all_gather(full_slices, 'space', axis=0, tiled=True)  136 us
    all_gather x1, waiting for transfers between devices, local(): full_slices = lax.all_gather(kernel_slices, 'vel', axis=2, tiled=True)  61.5 us
    dot_general x16, matrix products, one_slice(): lax.dot_general(matrix, source, (((0,), (0,)), ((), ())), preferred_eleme...  50.7 us
    ppermute x2, waiting for transfers between devices, extended(): before = lax.ppermute(last, axis, up)  38.2 us
    all_to_all x1, waiting for transfers between devices, local(): lax.all_to_all(summed, 'vel', split_axis=0, concat_axis=1, tiled=True)  29.2 us
    ppermute x2, starting transfers between devices, extended(): before = lax.ppermute(last, axis, up)  12.5 us
    all_to_all x1, waiting for transfers between devices, local(): lax.all_to_all(flattened, 'vel', split_axis=1, concat_axis=0, tiled=True)  10.2 us
  transfers between devices with their start and end apart: 8, of which 6 were waited for; matrix products, arithmetic and copies ran while one was open for 2% of the time, Pallas kernels for 0%

commit v1 on v0

--- a/solution.py
+++ b/solution.py
@@ -61,7 +61,10 @@
     upstream = jnp.where(forward, rebuilt_pad[:, :-2], rebuilt_pad[:, 2:])
     transported = density - courant[:, None, None, None] * (rebuilt - upstream)
     flattened = transported.astype(jnp.bfloat16).reshape(density.shape[0], -1)
-    columns = lax.all_to_all(flattened, "vel", split_axis=1, concat_axis=0, tiled=True)
+    columns = jnp.concatenate(
+        lax.all_to_all(jnp.stack(jnp.split(flattened, lax.axis_size("vel"), axis=1)), "vel", 0, 0),
+        axis=0,
+    )
     full_slices = lax.all_gather(kernel_slices, "vel", axis=2, tiled=True)
     initial = jnp.zeros(columns.shape, jnp.float32)
     summed = make_fold(columns, initial, lax.all_gather(full_slices, "space", axis=0, tiled=True))

time: 381 us -> 375 us (0.984)
  waiting for transfers between devices: 275 us -> 242 us
  blocking collectives: 0 us -> 29.7 us
  starting transfers between devices: 24.5 us -> 20.2 us
    all_to_all x0 -> x1, blocking collectives: none -> 29.7 us  [local(): lax.all_to_all(summed, 'vel', split_axis=0, concat_axis=1, tiled=True)]
    all_to_all x2 -> x1, waiting for transfers between devices: 39.4 us -> 10.1 us  [local(): lax.all_to_all(jnp.stack(jnp.split(flattened, lax.axis_size('vel'), axis=...]
    all_to_all x2 -> x1, starting transfers between devices: 8.03 us -> 3.56 us  [local(): lax.all_to_all(jnp.stack(jnp.split(flattened, lax.axis_size('vel'), axis=...]
    unnamed x13 -> x19, local copies, waits for them, and re-layouts: 7.26 us -> 9.46 us
  transfers between devices with their start and end apart: 8 -> 7, of which waited for: 6 -> 5; matrix products, arithmetic and copies ran while one was open for 2% -> 3% of each run, Pallas kernels for 0% -> 0%
where the time goes in v1:
time: 375 us; the launch traced here: 374 us
  waiting for transfers between devices  242 us (65%)
  matrix products  50.7 us (14%)
  blocking collectives  29.7 us (8%)
  starting transfers between devices  20.2 us (5%)
  between operations  14.2 us (4%)
  local copies, waits for them, and re-layouts  12.1 us (3%)
  other arithmetic  4.44 us (1%)
    all_gather x1, waiting for transfers between devices, local(): lax.all_gather(full_slices, 'space', axis=0, tiled=True)  133 us
    all_gather x1, waiting for transfers between devices, local(): full_slices = lax.all_gather(kernel_slices, 'vel', axis=2, tiled=True)  61.5 us
    dot_general x16, matrix products, one_slice(): lax.dot_general(matrix, source, (((0,), (0,)), ((), ())), preferred_eleme...  50.7 us
    ppermute x2, waiting for transfers between devices, extended(): before = lax.ppermute(last, axis, up)  36.7 us
    all_to_all x1, blocking collectives, local(): lax.all_to_all(summed, 'vel', split_axis=0, concat_axis=1, tiled=True)  29.7 us
    ppermute x2, starting transfers between devices, extended(): before = lax.ppermute(last, axis, up)  12.8 us
    all_to_all x1, waiting for transfers between devices, local(): lax.all_to_all(jnp.stack(jnp.split(flattened, lax.axis_size('vel'), axis=...  10.1 us
    unnamed x19, local copies, waits for them, and re-layouts  9.46 us
  transfers between devices with their start and end apart: 7, of which 5 were waited for; matrix products, arithmetic and copies ran while one was open for 3% of the time, Pallas kernels for 0%

profile of v1, /device:TPU:1, one launch (start us, length us, event | category | flops | bytes accessed | tf_op | source)
XLA Modules:
  0.0 373.6 jit_solution(5773291868022526601)
XLA Ops:
  8.0 61.5 %all-gather.3.cloned.1.call-done = bf16[1,1024,1024]{2,1,0:T(8,128)(2,1)} async-done(((bf16[1,1024,128]{2,1,0:T(8,128)(2,1)}), bf16[1,1024,1024]{2,1,0:T(8,128)(2,1)}) %all-gather.3.cloned.1.call-update) | async-done | bytes 2097168 | tf_op jit(solution)/shard_map/all_gather | solution.py:68
  69.6 6.6 %collective-permute-start = (f32[128,1,8,128]{3,2,1,0:T(8,128)S(1)}, f32[128,1,8,128]{3,2,1,0:T(8,128)S(1)}, u32[]{:S(2)}, u32[]{:S(2)}) collective-permute-start(f32[128,1,8,128]{3,2,1,0:T(8,128)S(1)} %get-tuple-element.111), channel_id=1, source_target_pairs={{0,1},{1,2},{2,3},{3,4},{4,5},{5,6},{6,7},{7,8},{8,9},{9,10},{10,1... | collective-permute-start | bytes 1572872 | tf_op jit(solution)/shard_map/ppermute | solution.py:17
  76.2 1.9 collective-permute-start.1
  78.2 10.1 %collective-permute-done = f32[128,1,8,128]{3,2,1,0:T(8,128)S(1)} collective-permute-done((f32[128,1,8,128]{3,2,1,0:T(8,128)S(1)}, f32[128,1,8,128]{3,2,1,0:T(8,128)S(1)}, u32[]{:S(2)}, u32[]{:S(2)}) %collective-permute-start) | collective-permute-done | bytes 524320 | tf_op jit(solution)/shard_map/ppermute | solution.py:17
  88.3 1.8 multiply_add_fusion
  90.1 6.2 %collective-permute-start.2 = (f32[128,1,8,128]{3,2,1,0:T(8,128)S(1)}, f32[128,1,8,128]{3,2,1,0:T(8,128)S(1)}, u32[]{:S(2)}, u32[]{:S(2)}) collective-permute-start(f32[128,1,8,128]{3,2,1,0:T(8,128)S(1)} %get-tuple-element.109), channel_id=1, source_target_pairs={{0,1},{1,2},{2,3},{3,4},{4,5},{5,6},{6,7},{7,8},{8,9},{9,10},{10,1... | collective-permute-start | bytes 1572872 | tf_op jit(solution)/shard_map/ppermute | solution.py:17
  96.3 1.9 collective-permute-start.3
  98.2 26.6 %collective-permute-done.2 = f32[128,1,8,128]{3,2,1,0:T(8,128)S(1)} collective-permute-done((f32[128,1,8,128]{3,2,1,0:T(8,128)S(1)}, f32[128,1,8,128]{3,2,1,0:T(8,128)S(1)}, u32[]{:S(2)}, u32[]{:S(2)}) %collective-permute-start.2) | collective-permute-done | bytes 524320 | tf_op jit(solution)/shard_map/ppermute | solution.py:17
  124.8 2.5 fusion.23
  133.1 3.6 all-to-all-start
  136.7 10.1 %all-to-all-done = bf16[8,128,512]{2,1,0:T(8,128)(2,1)S(1)} async-done(((bf16[8,128,512]{2,1,0:T(8,128)(2,1)}), bf16[8,128,512]{2,1,0:T(8,128)(2,1)S(1)}, u32[]{:S(2)}, u32[]{:S(2)}) %all-to-all-start) | async-done | bytes 1048608 | tf_op jit(solution)/shard_map/all_to_all | solution.py:65
  146.8 132.6 %all-gather.5.cloned.1.call-done = bf16[16,1024,1024]{2,1,0:T(8,128)(2,1)} async-done(((bf16[1,1024,1024]{2,1,0:T(8,128)(2,1)}), bf16[16,1024,1024]{2,1,0:T(8,128)(2,1)}) %all-gather.5.cloned.1.call-update) | async-done | bytes 33554448 | tf_op jit(solution)/shard_map/all_gather | solution.py:70
  279.4 51.4 %while.14 = (s32[]{:T(128)}, f32[1024,512]{1,0:T(8,128)S(1)}, bf16[1024,512]{1,0:T(8,128)(2,1)S(1)}, bf16[16,1024,1024]{2,1,0:T(8,128)(2,1)}, s32[]{:T(128)}, /*index=5*/s32[]{:T(128)}, s32[]{:T(128)}, s32[]{:T(128)}) while((s32[]{:T(128)}, f32[1024,512]{1,0:T(8,128)S(1)}, bf16[1024,512]{1,0:T(8,128)(2,1)S(1)}, ...), condition=%wide.region_1.2_spmd.clone, body=%wide.region_0.1_spmd.clone.sunk | while | flops 1075315200 | bytes 7345809 | solution.py:49
  279.4 3.2 select_add_fusion.2
  282.6 3.2 select_add_fusion.2
  285.9 3.2 select_add_fusion.2
  289.1 3.2 select_add_fusion.2
  292.3 3.2 select_add_fusion.2
  295.5 3.2 select_add_fusion.2
  298.7 3.2 select_add_fusion.2
  302.0 3.2 select_add_fusion.2
  305.2 3.2 select_add_fusion.2
  308.4 3.2 select_add_fusion.2
  311.6 3.2 select_add_fusion.2
  314.8 3.2 select_add_fusion.2
  318.0 3.2 select_add_fusion.2
  321.3 3.2 select_add_fusion.2
  324.5 3.2 select_add_fusion.2
  327.7 3.2 select_add_fusion.2
  332.2 29.7 %all_to_all.21 = f32[8,128,512]{2,1,0:T(8,128)S(1)} all-to-all(f32[8,128,512]{2,1,0:T(8,128)} %bitcast.65), channel_id=1, replica_groups=mesh['vel'=8,'space'=16] {'vel'}, dimensions={0} | all-to-all | bytes 4194304 | tf_op jit(solution)/shard_map/all_to_all | solution.py:71
  361.9 1.8 copy.8
  363.7 3.0 copy.9
  (47 shorter events, 8.2 us)
Async XLA Ops:
  7.2 62.3 %copy-start = (f32[128,4,8,128]{3,2,1,0:T(8,128)S(1)}, f32[128,4,8,128]{3,2,1,0:T(8,128)}, u32[]{:S(2)}) copy-start(f32[128,4,8,128]{3,2,1,0:T(8,128)} %param.7) | copy-start | bytes 6291460
  7.2 62.3 %all-gather.3.cloned.1.call-start = ((), (), s32[]{:S(2)}) async-start(), calls=%async_computation.2 | async-start | bytes 2359296 | tf_op jit(solution)/shard_map/all_gather | solution.py:68
  7.9 271.5 %all-gather.5.cloned.1.call-start = ((), (), s32[]{:S(2)}) async-start(), calls=%async_computation.3 | async-start | bytes 35651584 | tf_op jit(solution)/shard_map/all_gather | solution.py:70
  69.5 8.7 %copy-start.4 = (s32[128]{0:T(128)S(1)}, s32[128]{0:T(128)}, u32[]{:S(2)}) copy-start(s32[128]{0:T(128)} %param.9) | copy-start | bytes 1540
  69.5 8.7 %copy-start.2 = (s32[4,8,128]{2,1,0:T(8,128)S(1)}, s32[4,8,128]{2,1,0:T(8,128)}, u32[]{:S(2)}) copy-start(s32[4,8,128]{2,1,0:T(8,128)} %param.8) | copy-start | bytes 49156
  69.6 18.7 %collective-permute-start = (f32[128,1,8,128]{3,2,1,0:T(8,128)S(1)}, f32[128,1,8,128]{3,2,1,0:T(8,128)S(1)}, u32[]{:S(2)}, u32[]{:S(2)}) collective-permute-start(f32[128,1,8,128]{3,2,1,0:T(8,128)S(1)} %get-tuple-element.111), channel_id=1, source_target_pairs={{0,1},{1,2},{2,3},{3,4},{4,5},{5,6},{6,7},{7,8},{8,9},{9,10},{10,1... | collective-permute-start | bytes 1572872 | tf_op jit(solution)/shard_map/ppermute | solution.py:17
  76.2 12.1 %collective-permute-start.1 = (f32[128,1,8,128]{3,2,1,0:T(8,128)S(1)}, f32[128,1,8,128]{3,2,1,0:T(8,128)S(1)}, u32[]{:S(2)}, u32[]{:S(2)}) collective-permute-start(f32[128,1,8,128]{3,2,1,0:T(8,128)S(1)} %get-tuple-element.112), channel_id=1, source_target_pairs={{1,0},{2,1},{3,2},{4,3},{5,4},{6,5},{7,6},{8,7},{9,8},{10,9},{11,1... | collective-permute-start | bytes 1572872 | tf_op jit(solution)/shard_map/ppermute | solution.py:18
  90.0 34.8 %copy-start.3 = (f32[128]{0:T(128)S(1)}, f32[128]{0:T(128)}, u32[]{:S(2)}) copy-start(f32[128]{0:T(128)} %param.10) | copy-start | bytes 1540
  90.1 34.7 %collective-permute-start.2 = (f32[128,1,8,128]{3,2,1,0:T(8,128)S(1)}, f32[128,1,8,128]{3,2,1,0:T(8,128)S(1)}, u32[]{:S(2)}, u32[]{:S(2)}) collective-permute-start(f32[128,1,8,128]{3,2,1,0:T(8,128)S(1)} %get-tuple-element.109), channel_id=1, source_target_pairs={{0,1},{1,2},{2,3},{3,4},{4,5},{5,6},{6,7},{7,8},{8,9},{9,10},{10,1... | collective-permute-start | bytes 1572872 | tf_op jit(solution)/shard_map/ppermute | solution.py:17
  96.3 28.5 %collective-permute-start.3 = (f32[128,1,8,128]{3,2,1,0:T(8,128)S(1)}, f32[128,1,8,128]{3,2,1,0:T(8,128)S(1)}, u32[]{:S(2)}, u32[]{:S(2)}) collective-permute-start(f32[128,1,8,128]{3,2,1,0:T(8,128)S(1)} %get-tuple-element.110), channel_id=1, source_target_pairs={{1,0},{2,1},{3,2},{4,3},{5,4},{6,5},{7,6},{8,7},{9,8},{10,9},{11,1... | collective-permute-start | bytes 1572872 | tf_op jit(solution)/shard_map/ppermute | solution.py:18
  133.1 13.7 %all-to-all-start = ((bf16[8,128,512]{2,1,0:T(8,128)(2,1)}), bf16[8,128,512]{2,1,0:T(8,128)(2,1)S(1)}, u32[]{:S(2)}, u32[]{:S(2)}) async-start(bf16[8,128,512]{2,1,0:T(8,128)(2,1)} %fusion.15), calls=%async_computation | async-start | bytes 2097152 | tf_op jit(solution)/shard_map/all_to_all | solution.py:65
  330.9 1.3 copy-start.1
Sparse Core Ops, SparseCore 0:
  9.6 59.8 all-gather.2
  71.9 207.5 all-gather.4
